TPU v7x, 128 devices: a whole 4x4x4 slice. The times are simulated.
128 devices in a mesh: expert: 4 (over z), seq: 4 (over y), tensor: 8 (over x, core).
Axes of the slice: x: 4, y: 4, z: 4, core: 2. Of those that a mesh axis runs over, the one named last changes fastest.
Arguments:
- tokens: bfloat16 [3072, 7168], P(('expert', 'seq')), may hold values from -6 to 6
- grad_out: bfloat16 [3072, 7168], P(('expert', 'seq')), may hold values from -6 to 6
- expert_ids: int32 [3072, 2], P(('expert', 'seq')), may hold values from 0 to 3, all different within a row; in each aligned block of 192 rows (0 to 191, 192 to 383, ...) at most 128 rows name the same one
- route_weights: bfloat16 [3072, 2], P(('expert', 'seq')), may hold values from 0.099609375 to 1
- gate_weight: bfloat16 [4, 7168, 2048], P('expert', 'seq', 'tensor'), may hold values from -0.0625 to 0.0625
- up_weight: bfloat16 [4, 7168, 2048], P('expert', 'seq', 'tensor'), may hold values from -0.0625 to 0.0625
- down_weight: bfloat16 [4, 7168, 2048], P('expert', 'seq', 'tensor'), may hold values from -0.125 to 0.125
Outputs:
- grad_tokens: bfloat16 [3072, 7168], P(('expert', 'seq'), 'tensor')
- grad_route: float32 [3072, 2], P(('expert', 'seq'))
- grad_gate: float32 [4, 7168, 2048], P('expert', 'seq', 'tensor')
- grad_up: float32 [4, 7168, 2048], P('expert', 'seq', 'tensor')
- grad_down: float32 [4, 7168, 2048], P('expert', 'seq', 'tensor')
Inputs may be any that keep to these rules, and one draw needn't show every extreme that they name: `expert_ids`: the two ids of a row differ. Within each aligned block of 192 rows (the tokens of one group of the expert and seq axes) no expert is named by more than 128 rows, and in some block an expert is named by exactly 128 rows.
All inputs are finite; a program needn't handle non-finite values.
Results may differ from a plain program's by a relative error of at most 0.019.
Values may be sent and summed in bfloat16 or wider, within the bound.
A program may use at most 192 MiB of HBM per device.

v0:
```python
import jax
import jax.numpy as jnp
from jax import lax
from jax.sharding import PartitionSpec as P


def shards(tokens, grad_out, expert_ids, route_weights, gate_weight, up_weight, down_weight):
    expert_count = lax.axis_size("expert")
    seq_count = lax.axis_size("seq")
    tensor_count = lax.axis_size("tx") * lax.axis_size("core")
    core = lax.axis_index("core")
    local_count = gate_weight.shape[0]
    tok_rows = tokens.shape[0]
    model_width = tokens.shape[1]
    part_width = model_width // tensor_count
    per_peer = tok_rows // 6
    peer_count = expert_count * seq_count
    block_rows = local_count * per_peer
    slot_count = peer_count * block_rows
    flat_ids = expert_ids.reshape(-1)
    route_count = flat_ids.shape[0]
    onehot = (
        flat_ids[:, None] == jnp.arange(local_count * expert_count, dtype=jnp.int32)[None, :]
    ).astype(jnp.int32)
    before = jnp.cumsum(onehot, axis=0) - onehot
    ranking = jnp.sum(before * onehot, axis=1)
    local_expert = flat_ids % local_count
    dest_peer = flat_ids // local_count * seq_count + ranking % seq_count
    target = (dest_peer * local_count + local_expert) * per_peer + ranking // seq_count
    source = (
        jnp.full((slot_count,), -1, jnp.int32)
        .at[target]
        .set(jnp.arange(route_count, dtype=jnp.int32))
    )
    filled = source >= 0
    safe_source = jnp.maximum(source, 0)
    token_of = safe_source // 2
    keep = filled[:, None].astype(tokens.dtype)
    weight_send = (
        route_weights.reshape(-1)[safe_source] * filled.astype(route_weights.dtype)
    ).reshape(peer_count, block_rows)
    half = model_width // 2
    tokens_half = lax.dynamic_slice_in_dim(tokens, core * half, half, axis=1)
    grad_half = lax.dynamic_slice_in_dim(grad_out, core * half, half, axis=1)
    in_send = (tokens_half[token_of] * keep).reshape(peer_count, block_rows, half)
    out_send = (grad_half[token_of] * keep).reshape(peer_count, block_rows, half)
    in_mine, out_mine, weight_recv = (
        lax.all_to_all(in_send, ("expert", "seq"), split_axis=0, concat_axis=0, tiled=True),
        lax.all_to_all(out_send, ("expert", "seq"), split_axis=0, concat_axis=0, tiled=True),
        lax.all_to_all(weight_send, ("expert", "seq"), split_axis=0, concat_axis=0, tiled=True),
    )

    def join_halves(mine):
        other = lax.ppermute(mine, "core", [(0, 1), (1, 0)])
        first = jnp.where(core == 0, mine, other)
        second = jnp.where(core == 0, other, mine)
        return jnp.concatenate([first, second], axis=-1)

    in_recv = join_halves(in_mine)
    out_recv = join_halves(out_mine)

    def by_expert(values):
        shaped = values.reshape((peer_count, local_count, per_peer) + values.shape[2:])
        return jnp.swapaxes(shaped, 0, 1).reshape(
            (local_count, peer_count * per_peer) + values.shape[2:]
        )

    def by_peer(values):
        shaped = values.reshape((local_count, peer_count, per_peer) + values.shape[2:])
        return jnp.swapaxes(shaped, 0, 1).reshape((peer_count, block_rows) + values.shape[2:])

    in_rows = by_expert(in_recv)
    out_rows = by_expert(out_recv)
    prob = by_expert(weight_recv).astype(jnp.float32)[:, :, None]
    gate_full, up_full, down_full = (
        lax.all_gather(gate_weight, "seq", axis=1, tiled=True),
        lax.all_gather(up_weight, "seq", axis=1, tiled=True),
        lax.all_gather(down_weight, "seq", axis=1, tiled=True),
    )
    pre_gate = jnp.einsum("emd,edf->emf", in_rows, gate_full, preferred_element_type=jnp.float32)
    pre_up = jnp.einsum("emd,edf->emf", in_rows, up_full, preferred_element_type=jnp.float32)
    sigmoid_gate = jax.nn.sigmoid(pre_gate)
    silu_gate = pre_gate * sigmoid_gate
    hidden = silu_gate * pre_up
    hidden_low = hidden.astype(jnp.bfloat16)
    back_proj = jnp.einsum("emd,edf->emf", out_rows, down_full, preferred_element_type=jnp.float32)
    partial_scores = jnp.sum(hidden * back_proj, axis=2)
    scaled = (prob * out_rows.astype(jnp.float32)).astype(jnp.bfloat16)
    hidden_grad = prob * back_proj
    up_grad = (hidden_grad * silu_gate).astype(jnp.bfloat16)
    gate_grad = (
        hidden_grad * pre_up * sigmoid_gate * (1.0 + pre_gate * (1.0 - sigmoid_gate))
    ).astype(jnp.bfloat16)
    input_terms = jnp.einsum(
        "emf,edf->emd", gate_grad, gate_full, preferred_element_type=jnp.float32
    )
    input_terms = input_terms + jnp.einsum(
        "emf,edf->emd", up_grad, up_full, preferred_element_type=jnp.float32
    )
    route_scores = lax.psum(partial_scores, ("tx", "core"))
    input_shards = lax.psum_scatter(
        input_terms.astype(jnp.bfloat16), ("tx", "core"), scatter_dimension=2, tiled=True
    ).astype(jnp.float32)
    back_rows, back_scores = (
        lax.all_to_all(
            by_peer(input_shards).astype(jnp.bfloat16),
            ("expert", "seq"),
            split_axis=0,
            concat_axis=0,
            tiled=True,
        ).astype(jnp.float32),
        lax.all_to_all(
            by_peer(route_scores).astype(jnp.bfloat16),
            ("expert", "seq"),
            split_axis=0,
            concat_axis=0,
            tiled=True,
        ).astype(jnp.float32),
    )
    route_rows = back_rows.reshape(slot_count, part_width)[target].reshape(tok_rows, 2, part_width)
    grad_tokens = jnp.sum(route_rows, axis=1).astype(jnp.bfloat16)
    grad_route = back_scores.reshape(slot_count)[target].reshape(tok_rows, 2)
    gate_part = jnp.einsum("emd,emf->edf", in_rows, gate_grad, preferred_element_type=jnp.float32)
    up_part = jnp.einsum("emd,emf->edf", in_rows, up_grad, preferred_element_type=jnp.float32)
    down_part = jnp.einsum("emd,emf->edf", scaled, hidden_low, preferred_element_type=jnp.float32)
    grad_gate, grad_up, grad_down = (
        lax.psum_scatter(
            gate_part.astype(jnp.bfloat16), "seq", scatter_dimension=1, tiled=True
        ).astype(jnp.float32),
        lax.psum_scatter(
            up_part.astype(jnp.bfloat16), "seq", scatter_dimension=1, tiled=True
        ).astype(jnp.float32),
        lax.psum_scatter(
            down_part.astype(jnp.bfloat16), "seq", scatter_dimension=1, tiled=True
        ).astype(jnp.float32),
    )
    return (grad_tokens, grad_route, grad_gate, grad_up, grad_down)


def solution(mesh):
    shape = mesh.devices.shape
    mesh = jax.sharding.Mesh(
        mesh.devices.reshape(shape[0], shape[1], shape[2] // 2, 2), ("expert", "seq", "tx", "core")
    )
    tensor = ("tx", "core")
    placed = (
        P(("expert", "seq"), None),
        P(("expert", "seq"), None),
        P(("expert", "seq"), None),
        P(("expert", "seq"), None),
        P("expert", "seq", tensor),
        P("expert", "seq", tensor),
        P("expert", "seq", tensor),
    )
    return jax.shard_map(
        shards,
        mesh=mesh,
        in_specs=placed,
        out_specs=(
            P(("expert", "seq"), tensor),
            P(("expert", "seq"), None),
            P("expert", "seq", tensor),
            P("expert", "seq", tensor),
            P("expert", "seq", tensor),
        ),
        check_vma=False,
    )
```

profile of v0, /device:TPU:1, one launch (start us, length us, event | category | flops | bytes accessed | tf_op | source)
XLA Modules:
  0.0 511.5 jit_solution(3057996658511665825)
XLA Ops:
  7.2 0.7 all-gather.8.cloned.1.call-update
  7.9 0.8 copy.24
  8.7 0.1 eq.38
  8.8 0.1 eq.34
  9.0 0.8 copy.26
  9.8 0.2 reshape.290
  10.0 0.7 broadcast_multiply_fusion.2
  10.7 0.1 copy.23
  10.8 0.1 mul.119
  11.0 1.2 reduce-window.6
  12.2 0.2 slice_reduce_fusion
  12.4 0.2 reduce-window.9
  12.7 2.9 scatter_custom_fusion
  15.7 3.5 gather_fusion
  19.2 0.1 reshape.301
  19.3 1.9 constant_dynamic-slice_fusion
  21.2 4.2 gather_fusion.2
  25.4 4.2 gather_fusion.1
  29.6 6.8 %broadcast_multiply_fusion.1 = (bf16[16,32,3584]{2,1,0:T(8,128)(2,1)}, bf16[16,32,3584]{2,1,0:T(8,128)(2,1)}) fusion(bf16[16,32,3584]{2,1,0:T(8,128)(2,1)} %bitcast.74, bf16[16,32]{1,0:T(8,128)(2,1)S(1)} %reshape.301, bf16[16,32,3584]{2,1,0:T(8,128)(2,1)} %bitcast.73), kind=kLoop, calls=%fused_computation.34 | loop fusion | flops 3670016 | bytes 14681088 | tf_op jit(solution)/shard_map/mul | solution.py:46
  36.4 8.9 %all-to-all-start.2 = ((bf16[16,32,3584]{2,1,0:T(8,128)(2,1)}), bf16[16,32,3584]{2,1,0:T(8,128)(2,1)}, u32[]{:S(2)}, u32[]{:S(2)}) async-start(bf16[16,32,3584]{2,1,0:T(8,128)(2,1)} %get-tuple-element.30), calls=%async_computation.2 | async-start | bytes 7340032 | tf_op jit(solution)/shard_map/all_to_all | solution.py:48
  45.3 0.7 all-gather.6.cloned.1.call-update
  46.0 70.6 %all-to-all-done.2 = bf16[16,32,3584]{2,1,0:T(8,128)(2,1)} async-done(((bf16[16,32,3584]{2,1,0:T(8,128)(2,1)}), bf16[16,32,3584]{2,1,0:T(8,128)(2,1)}, u32[]{:S(2)}, u32[]{:S(2)}) %all-to-all-start.2) | async-done | bytes 3670048 | tf_op jit(solution)/shard_map/all_to_all | solution.py:48
  116.7 1.8 collective-permute-start.1
  118.5 0.1 all_to_all.25
  118.6 11.5 %all_to_all.31 = bf16[16,1,32]{2,1,0:T(2,128)(2,1)S(1)} all-to-all(bf16[16,1,32]{2,1,0:T(2,128)(2,1)S(1)} %all_to_all.25), channel_id=1, replica_groups=mesh['expert'=4,'seq'=4,'tx'=4,'core'=2] {'expert','seq'}, dimensions={0} | all-to-all | bytes 2048 | tf_op jit(solution)/shard_map/all_to_all | solution.py:50
  130.1 4.5 all-to-all-start.1
  134.7 0.7 all-gather.4.cloned.1.call-update
  135.4 0.1 reshape.300
  135.5 64.9 %all-to-all-done.1 = bf16[16,32,3584]{2,1,0:T(8,128)(2,1)} async-done(((bf16[16,32,3584]{2,1,0:T(8,128)(2,1)}), bf16[16,32,3584]{2,1,0:T(8,128)(2,1)}, u32[]{:S(2)}, u32[]{:S(2)}) %all-to-all-start.1) | async-done | bytes 3670048 | tf_op jit(solution)/shard_map/all_to_all | solution.py:49
  200.5 6.6 %collective-permute-start = (bf16[16,32,3584]{2,1,0:T(8,128)(2,1)}, bf16[16,32,3584]{2,1,0:T(8,128)(2,1)}, u32[]{:S(2)}, u32[]{:S(2)}) collective-permute-start(bf16[16,32,3584]{2,1,0:T(8,128)(2,1)} %all-to-all-done.1), channel_id=1, source_target_pairs={{0,1},{1,0},{2,3},{3,2},{4,5},{5,4},{6,7},{7,6},{8,9},{9,8},{10,11... | collective-permute-start | bytes 11010056 | tf_op jit(solution)/shard_map/ppermute | solution.py:54
  207.0 5.4 %broadcast_select_fusion.1 = (bf16[16,32,3584]{2,1,0:T(8,128)(2,1)S(1)}, bf16[16,32,3584]{2,1,0:T(8,128)(2,1)}) fusion(bf16[16,32,3584]{2,1,0:T(8,128)(2,1)} %all-to-all-done.2, bf16[16,32,3584]{2,1,0:T(8,128)(2,1)} %collective-permute-done.1, pred[]{:T(512)S(6)} %eq.42), kind=kLoop, calls=%fused_computation.29 | loop fusion | flops 3670016 | bytes 14680065 | tf_op jit(solution)/shard_map/jit(_where)/select_n | solution.py:55
  212.5 5.8 %pad_maximum_fusion.1 = bf16[16,32,7168]{2,1,0:T(8,128)(2,1)} fusion(bf16[16,32,3584]{2,1,0:T(8,128)(2,1)} %get-tuple-element.25, bf16[16,32,3584]{2,1,0:T(8,128)(2,1)S(1)} %get-tuple-element.24), kind=kLoop, calls=%fused_computation.16 | loop fusion | flops 14680064 | bytes 14680064 | tf_op jit(solution)/shard_map/concatenate | solution.py:57
  218.2 6.2 %fusion.7 = f32[512,256]{0,1:T(8,128)S(1)} fusion(bf16[512,7168]{1,0:T(8,128)(2,1)} %bitcast.67, bf16[1,7168,256]{2,1,0:T(8,128)(2,1)} %all-gather.8.cloned.1.call-done), kind=kOutput, calls=%fused_computation.21 | convolution fusion | flops 1879048192 | bytes 11534336 | tf_op jit(solution)/shard_map/emd,edf->emf/dot_general | solution.py:80
  224.5 6.2 %fusion.10 = f32[512,256]{0,1:T(8,128)S(1)} fusion(bf16[512,7168]{1,0:T(8,128)(2,1)} %bitcast.68, bf16[1,7168,256]{2,1,0:T(8,128)(2,1)} %all-gather.6.cloned.1.call-done), kind=kOutput, calls=%fused_computation.24 | convolution fusion | flops 1879048192 | bytes 11534336 | tf_op jit(solution)/shard_map/emd,edf->emf/dot_general | solution.py:81
  230.7 5.6 %broadcast_select_fusion.3 = (bf16[16,32,3584]{2,1,0:T(8,128)(2,1)S(1)}, bf16[16,32,3584]{2,1,0:T(8,128)(2,1)}) fusion(bf16[16,32,3584]{2,1,0:T(8,128)(2,1)} %all-to-all-done.1, bf16[16,32,3584]{2,1,0:T(8,128)(2,1)} %collective-permute-done, pred[]{:T(512)S(6)} %eq.42), kind=kLoop, calls=%fused_computation.31 | loop fusion | flops 3670016 | bytes 14680065 | tf_op jit(solution)/shard_map/jit(_where)/select_n | solution.py:55
  236.3 5.8 %pad_maximum_fusion = bf16[16,32,7168]{2,1,0:T(8,128)(2,1)} fusion(bf16[16,32,3584]{2,1,0:T(8,128)(2,1)} %get-tuple-element.23, bf16[16,32,3584]{2,1,0:T(8,128)(2,1)S(1)} %get-tuple-element.22), kind=kLoop, calls=%fused_computation.15 | loop fusion | flops 14680064 | bytes 14680064 | tf_op jit(solution)/shard_map/concatenate | solution.py:57
  242.1 6.6 %multiply_reduce_fusion = (f32[512]{0:T(512)S(1)}, bf16[512,256]{0,1:T(8,128)(2,1)S(1)}, bf16[512,256]{0,1:T(8,128)(2,1)S(1)}) fusion(f32[512,256]{0,1:T(8,128)S(1)} %fusion.10, f32[512,256]{0,1:T(8,128)S(1)} %fusion.7, f32[512]{0:T(512)S(1)} %reshape.300, bf16[512,7168]{1,0:T(8,128)(2,1)} %bitcast.75, bf16[1,7168,256]{2,1,0:T(8,128)(2,1)} %all-gather.4.cloned.1.call-done), kind=kOutput, calls=%fused_computation.36 | convolution fusion | flops 1881275904 | bytes 12587008 | tf_op jit(solution)/shard_map/emd,edf->emf/dot_general | solution.py:86
  248.7 7.3 %fusion.5 = f32[512,7168]{1,0:T(8,128)} fusion(bf16[512,256]{0,1:T(8,128)(2,1)S(1)} %get-tuple-element.27, bf16[1,7168,256]{2,1,0:T(8,128)(2,1)S(1)} %copy-done.1), kind=kOutput, calls=%fused_computation.19 | convolution fusion | flops 1879048192 | bytes 18612224 | tf_op jit(solution)/shard_map/emf,edf->emd/dot_general | solution.py:94
  256.0 10.6 %fusion = bf16[1,512,7168]{2,1,0:T(8,128)(2,1)} fusion(f32[512,7168]{1,0:T(8,128)} %fusion.5, bf16[512,256]{0,1:T(8,128)(2,1)S(1)} %get-tuple-element.28, bf16[1,7168,256]{2,1,0:T(8,128)(2,1)S(1)} %copy-done), kind=kOutput, calls=%fused_computation.8 | convolution fusion | flops 1886388224 | bytes 25952256 | tf_op jit(solution)/shard_map/emf,edf->emd/dot_general | solution.py:97
  266.6 31.4 %copy.30 = bf16[1,512,7168]{1,0,2:T(2,128)(2,1)} copy(bf16[1,512,7168]{2,1,0:T(8,128)(2,1)} %fusion) | data formatting | bytes 14680064
  298.1 10.3 %copy.36 = bf16[7168,1,512]{2,0,1:T(8,128)(2,1)} copy(bf16[7168,1,512]{2,1,0:T(2,128)(2,1)} %bitcast.71) | data formatting | bytes 14680064
  308.5 8.0 %fusion.3 = bf16[1,7168,256]{2,1,0:T(8,128)(2,1)} fusion(bf16[512,7168]{1,0:T(8,128)(2,1)} %bitcast.76, f32[512]{0:T(512)S(1)} %reshape.300, f32[512,256]{0,1:T(8,128)S(1)} %fusion.10, f32[512,256]{0,1:T(8,128)S(1)} %fusion.7), kind=kOutput, calls=%fused_computation.14 | convolution fusion | flops 1892679680 | bytes 12060672 | tf_op jit(solution)/shard_map/emd,emf->edf/dot_general | solution.py:125
  316.6 7.1 %fusion.1 = bf16[1,7168,256]{2,1,0:T(8,128)(2,1)} fusion(bf16[512,7168]{1,0:T(8,128)(2,1)} %bitcast.69, bf16[512,256]{0,1:T(8,128)(2,1)S(1)} %get-tuple-element.27), kind=kOutput, calls=%fused_computation.12 | convolution fusion | flops 1880883200 | bytes 11272192 | tf_op jit(solution)/shard_map/emd,emf->edf/dot_general | solution.py:123
  323.8 7.2 %fusion.2 = bf16[1,7168,256]{2,1,0:T(8,128)(2,1)} fusion(bf16[512,7168]{1,0:T(8,128)(2,1)} %bitcast.70, bf16[512,256]{0,1:T(8,128)(2,1)S(1)} %get-tuple-element.28), kind=kOutput, calls=%fused_computation.13 | convolution fusion | flops 1880883200 | bytes 11272192 | tf_op jit(solution)/shard_map/emd,emf->edf/dot_general | solution.py:124
  330.9 23.5 %psum.7 = bf16[1,512]{1,0:T(2,128)(2,1)S(1)} all-reduce(f32[1,512]{1,0:T(1,128)S(1)} %bitcast.78), channel_id=1, replica_groups=mesh['expert'=4,'seq'=4,'tx'=4,'core'=2] {'tx','core'}, use_global_device_ids=true, to_apply=%region_7.8 | all-reduce | flops 512 | bytes 3072 | tf_op jit(solution)/shard_map/psum | solution.py:100
  354.4 0.7 convert_element_type.144
  355.1 3.7 all-to-all-start.4
  358.9 2.1 reshape_bitcast_fusion
  361.0 3.4 copy.31
  364.4 0.7 all-to-all-done.4
  365.1 6.0 %all-to-all-start.3 = ((bf16[16,32,896]{2,1,0:T(8,128)(2,1)}), bf16[16,32,896]{2,1,0:T(8,128)(2,1)S(1)}, u32[]{:S(2)}, u32[]{:S(2)}) async-start(bf16[16,32,896]{2,1,0:T(8,128)(2,1)} %bitcast.9), calls=%async_computation.3 | async-start | bytes 1835008 | tf_op jit(solution)/shard_map/all_to_all | solution.py:105
  371.2 2.8 gather_fusion.4
  374.0 0.1 reshape.299
  374.1 0.7 copy.29
  374.8 32.5 %reduce-scatter.11.cloned.1.call-done = bf16[1,1792,256]{2,1,0:T(8,128)(2,1)} async-done(((bf16[1,7168,256]{2,1,0:T(8,128)(2,1)}), bf16[1,1792,256]{2,1,0:T(8,128)(2,1)}) %reduce-scatter.11.cloned.1.call-update) | async-done | bytes 917520 | tf_op jit(solution)/shard_map/reduce_scatter | solution.py:133
  407.3 2.5 convert_element_type.141
  409.9 41.9 %reduce-scatter.7.cloned.1.call-done = bf16[1,1792,256]{2,1,0:T(8,128)(2,1)} async-done(((bf16[1,7168,256]{2,1,0:T(8,128)(2,1)}), bf16[1,1792,256]{2,1,0:T(8,128)(2,1)}) %reduce-scatter.7.cloned.1.call-update) | async-done | bytes 917520 | tf_op jit(solution)/shard_map/reduce_scatter | solution.py:127
  451.7 2.5 convert_element_type.132
  454.3 42.1 %reduce-scatter.9.cloned.1.call-done = bf16[1,1792,256]{2,1,0:T(8,128)(2,1)} async-done(((bf16[1,7168,256]{2,1,0:T(8,128)(2,1)}), bf16[1,1792,256]{2,1,0:T(8,128)(2,1)}) %reduce-scatter.9.cloned.1.call-update) | async-done | bytes 917520 | tf_op jit(solution)/shard_map/reduce_scatter | solution.py:130
  496.4 2.5 convert_element_type.135
  499.0 0.2 bitcast_convert_fusion
  499.2 1.9 gather_fusion.3
  501.1 0.8 reshape.298
  501.9 2.5 reduce_sum.33
  (36 shorter events, 0.7 us)
Async XLA Ops:
  7.2 211.1 %all-gather.8.cloned.1.call-start = ((), (), s32[]{:S(2)}) async-start(), calls=%async_computation.11 | async-start | bytes 4587520 | tf_op jit(solution)/shard_map/all_gather | solution.py:76
  36.4 80.3 %all-to-all-start.2 = ((bf16[16,32,3584]{2,1,0:T(8,128)(2,1)}), bf16[16,32,3584]{2,1,0:T(8,128)(2,1)}, u32[]{:S(2)}, u32[]{:S(2)}) async-start(bf16[16,32,3584]{2,1,0:T(8,128)(2,1)} %get-tuple-element.30), calls=%async_computation.2 | async-start | bytes 7340032 | tf_op jit(solution)/shard_map/all_to_all | solution.py:48
  45.3 179.2 %all-gather.6.cloned.1.call-start = ((), (), s32[]{:S(2)}) async-start(), calls=%async_computation.10 | async-start | bytes 4587520 | tf_op jit(solution)/shard_map/all_gather | solution.py:77
  116.7 90.4 %collective-permute-start.1 = (bf16[16,32,3584]{2,1,0:T(8,128)(2,1)}, bf16[16,32,3584]{2,1,0:T(8,128)(2,1)}, u32[]{:S(2)}, u32[]{:S(2)}) collective-permute-start(bf16[16,32,3584]{2,1,0:T(8,128)(2,1)} %all-to-all-done.2), channel_id=1, source_target_pairs={{0,1},{1,0},{2,3},{3,2},{4,5},{5,4},{6,7},{7,6},{8,9},{9,8},{10,11... | collective-permute-start | bytes 11010056 | tf_op jit(solution)/shard_map/ppermute | solution.py:54
  130.1 70.3 %all-to-all-start.1 = ((bf16[16,32,3584]{2,1,0:T(8,128)(2,1)}), bf16[16,32,3584]{2,1,0:T(8,128)(2,1)}, u32[]{:S(2)}, u32[]{:S(2)}) async-start(bf16[16,32,3584]{2,1,0:T(8,128)(2,1)} %get-tuple-element.29), calls=%async_computation.1 | async-start | bytes 7340032 | tf_op jit(solution)/shard_map/all_to_all | solution.py:49
  134.6 107.4 %all-gather.4.cloned.1.call-start = ((), (), s32[]{:S(2)}) async-start(), calls=%async_computation.9 | async-start | bytes 4587520 | tf_op jit(solution)/shard_map/all_gather | solution.py:78
  135.4 223.5 %reduce-scatter.13.cloned.1.call-start = ((), (), s32[]{:S(2)}) async-start(), calls=%async_computation.15 | async-start | bytes 8257536
  200.5 30.3 %collective-permute-start = (bf16[16,32,3584]{2,1,0:T(8,128)(2,1)}, bf16[16,32,3584]{2,1,0:T(8,128)(2,1)}, u32[]{:S(2)}, u32[]{:S(2)}) collective-permute-start(bf16[16,32,3584]{2,1,0:T(8,128)(2,1)} %all-to-all-done.1), channel_id=1, source_target_pairs={{0,1},{1,0},{2,3},{3,2},{4,5},{5,4},{6,7},{7,6},{8,9},{9,8},{10,11... | collective-permute-start | bytes 11010056 | tf_op jit(solution)/shard_map/ppermute | solution.py:54
  242.1 6.6 %copy-start.1 = (bf16[1,7168,256]{2,1,0:T(8,128)(2,1)S(1)}, bf16[1,7168,256]{2,1,0:T(8,128)(2,1)}, u32[]{:S(2)}) copy-start(bf16[1,7168,256]{2,1,0:T(8,128)(2,1)} %all-gather.8.cloned.1.call-done) | copy-start | bytes 11010052
  248.7 7.4 %copy-start = (bf16[1,7168,256]{2,1,0:T(8,128)(2,1)S(1)}, bf16[1,7168,256]{2,1,0:T(8,128)(2,1)}, u32[]{:S(2)}) copy-start(bf16[1,7168,256]{2,1,0:T(8,128)(2,1)} %all-gather.6.cloned.1.call-done) | copy-start | bytes 11010052
  308.4 98.9 %reduce-scatter.11.cloned.1.call-start = ((), (), s32[]{:S(2)}) async-start(), calls=%async_computation.14 | async-start | bytes 4587520 | tf_op jit(solution)/shard_map/reduce_scatter | solution.py:133
  316.5 135.2 %reduce-scatter.7.cloned.1.call-start = ((), (), s32[]{:S(2)}) async-start(), calls=%async_computation.12 | async-start | bytes 4587520 | tf_op jit(solution)/shard_map/reduce_scatter | solution.py:127
  323.7 172.7 %reduce-scatter.9.cloned.1.call-start = ((), (), s32[]{:S(2)}) async-start(), calls=%async_computation.13 | async-start | bytes 4587520 | tf_op jit(solution)/shard_map/reduce_scatter | solution.py:130
  355.1 9.9 %all-to-all-start.4 = ((bf16[16,1,32]{2,1,0:T(2,128)(2,1)}), bf16[16,1,32]{2,1,0:T(2,128)(2,1)S(1)}, u32[]{:S(2)}, u32[]{:S(2)}) async-start(bf16[16,1,32]{2,1,0:T(2,128)(2,1)} %convert_element_type.144), calls=%async_computation.4 | async-start | bytes 16384 | tf_op jit(solution)/shard_map/all_to_all | solution.py:112
  365.1 133.9 %all-to-all-start.3 = ((bf16[16,32,896]{2,1,0:T(8,128)(2,1)}), bf16[16,32,896]{2,1,0:T(8,128)(2,1)S(1)}, u32[]{:S(2)}, u32[]{:S(2)}) async-start(bf16[16,32,896]{2,1,0:T(8,128)(2,1)} %bitcast.9), calls=%async_computation.3 | async-start | bytes 1835008 | tf_op jit(solution)/shard_map/all_to_all | solution.py:105
Sparse Core Ops, SparseCore 0:
  9.7 68.7 all-gather.7
  80.2 55.4 all-gather.5
  137.3 70.2 all-gather.3
  308.6 43.6 reduce-scatter.12
  354.5 52.7 reduce-scatter.10
  409.6 42.1 reduce-scatter.6
  454.2 42.2 reduce-scatter.8
where the time goes:
time: 519 us; the launch traced here: 512 us
  waiting for transfers between devices  255 us (49%)
  local copies, waits for them, and re-layouts  73.9 us (14%)
  matrix products  59.3 us (11%)
  other arithmetic  42 us (8%)
  blocking collectives  35 us (7%)
  starting transfers between devices  31.7 us (6%)
  between operations  14.6 us (3%)
    all_to_all x1, waiting for transfers between devices, shards(): lax.all_to_all(in_send, ('expert', 'seq'), split_axis=0, concat_axis=0, t...  70.6 us
    all_to_all x1, waiting for transfers between devices, shards(): lax.all_to_all(out_send, ('expert', 'seq'), split_axis=0, concat_axis=0,...  64.9 us
    unnamed x11, local copies, waits for them, and re-layouts  49.6 us
    reduce_scatter x1, waiting for transfers between devices, shards(): lax.psum_scatter(up_part.astype(jnp.bfloat16), 'seq', scatter_dimension=1...  42.1 us
    reduce_scatter x1, waiting for transfers between devices, shards(): lax.psum_scatter(gate_part.astype(jnp.bfloat16), 'seq', scatter_dimension...  41.9 us
    reduce_scatter x1, waiting for transfers between devices, shards(): lax.psum_scatter(down_part.astype(jnp.bfloat16), 'seq', scatter_dimension...  32.5 us
    psum x1, blocking collectives, shards(): route_scores = lax.psum(partial_scores, ('tx', 'core'))  23.5 us
    all_to_all x1, blocking collectives, shards(): lax.all_to_all(weight_send, ('expert', 'seq'), split_axis=0, concat_axis=...  11.5 us
  transfers between devices with their start and end apart: 13, of which 6 were waited for; matrix products, arithmetic and copies ran while one was open for 20% of the time, Pallas kernels for 0%

commit v1 on v0

--- a/solution.py
+++ b/solution.py
@@ -2,9 +2,16 @@
 import jax.numpy as jnp
 from jax import lax
 from jax.sharding import PartitionSpec as P
+from jax.lax import psum
 
 
 def shards(tokens, grad_out, expert_ids, route_weights, gate_weight, up_weight, down_weight):
+
+    def part_the_stops_all(vals, along_axis, chip_axis):
+        kept_arr = psum(vals, along_axis)
+        side_arr = psum(kept_arr, chip_axis)
+        return side_arr
+
     expert_count = lax.axis_size("expert")
     seq_count = lax.axis_size("seq")
     tensor_count = lax.axis_size("tx") * lax.axis_size("core")
@@ -97,7 +104,7 @@
     input_terms = input_terms + jnp.einsum(
         "emf,edf->emd", up_grad, up_full, preferred_element_type=jnp.float32
     )
-    route_scores = lax.psum(partial_scores, ("tx", "core"))
+    route_scores = part_the_stops_all(partial_scores, "tx", "core")
     input_shards = lax.psum_scatter(
         input_terms.astype(jnp.bfloat16), ("tx", "core"), scatter_dimension=2, tiled=True
     ).astype(jnp.float32)

time: 519 us -> 519 us (level)
  blocking collectives: 35 us -> 25.6 us
  waiting for transfers between devices: 255 us -> 264 us
    psum x1 -> x2, blocking collectives: 23.5 us -> 14.1 us  [the longest x1 9.36 us: part_the_stops_all(): kept_arr = psum(vals, along_axis)]
    reduce_scatter x1, waiting for transfers between devices: 32.5 us -> 39.1 us  [shards(): lax.psum_scatter(down_part.astype(jnp.bfloat16), 'seq', scatter_dimension...]
where the time goes in v1:
time: 519 us; the launch traced here: 512 us
  waiting for transfers between devices  264 us (51%)
  local copies, waits for them, and re-layouts  73.9 us (14%)
  matrix products  59.3 us (11%)
  other arithmetic  42 us (8%)
  starting transfers between devices  32.5 us (6%)
  blocking collectives  25.6 us (5%)
  between operations  14.6 us (3%)
    all_to_all x1, waiting for transfers between devices, shards(): lax.all_to_all(in_send, ('expert', 'seq'), split_axis=0, concat_axis=0, t...  70.6 us
    all_to_all x1, waiting for transfers between devices, shards(): lax.all_to_all(out_send, ('expert', 'seq'), split_axis=0, concat_axis=0,...  64.9 us
    unnamed x11, local copies, waits for them, and re-layouts  49.6 us
    reduce_scatter x1, waiting for transfers between devices, shards(): lax.psum_scatter(up_part.astype(jnp.bfloat16), 'seq', scatter_dimension=1...  42.1 us
    reduce_scatter x1, waiting for transfers between devices, shards(): lax.psum_scatter(gate_part.astype(jnp.bfloat16), 'seq', scatter_dimension...  42 us
    reduce_scatter x1, waiting for transfers between devices, shards(): lax.psum_scatter(down_part.astype(jnp.bfloat16), 'seq', scatter_dimension...  39.1 us
    all_to_all x1, blocking collectives, shards(): lax.all_to_all(weight_send, ('expert', 'seq'), split_axis=0, concat_axis=...  11.5 us
    concatenate x2, other arithmetic, join_halves(): return jnp.concatenate([first, second], axis=-1)  11.5 us
  transfers between devices with their start and end apart: 13, of which 6 were waited for; matrix products, arithmetic and copies ran while one was open for 20% of the time, Pallas kernels for 0%

profile of v1, /device:TPU:1, one launch (start us, length us, event | category | flops | bytes accessed | tf_op | source)
XLA Modules:
  0.0 511.5 jit_solution(17637828552959129799)
XLA Ops:
  7.2 0.7 all-gather.8.cloned.1.call-update
  7.9 0.8 copy.24
  8.7 0.1 eq.38
  8.8 0.1 eq.34
  9.0 0.8 copy.26
  9.8 0.2 reshape.290
  10.0 0.7 broadcast_multiply_fusion.2
  10.7 0.1 copy.23
  10.8 0.1 mul.119
  11.0 1.2 reduce-window.6
  12.2 0.2 slice_reduce_fusion
  12.4 0.2 reduce-window.9
  12.7 2.9 scatter_custom_fusion
  15.7 3.5 gather_fusion
  19.2 0.1 reshape.301
  19.3 1.9 constant_dynamic-slice_fusion
  21.2 4.2 gather_fusion.2
  25.4 4.2 gather_fusion.1
  29.6 6.8 %broadcast_multiply_fusion.1 = (bf16[16,32,3584]{2,1,0:T(8,128)(2,1)}, bf16[16,32,3584]{2,1,0:T(8,128)(2,1)}) fusion(bf16[16,32,3584]{2,1,0:T(8,128)(2,1)} %bitcast.74, bf16[16,32]{1,0:T(8,128)(2,1)S(1)} %reshape.301, bf16[16,32,3584]{2,1,0:T(8,128)(2,1)} %bitcast.73), kind=kLoop, calls=%fused_computation.34 | loop fusion | flops 3670016 | bytes 14681088 | tf_op jit(solution)/shard_map/mul | solution.py:53
  36.4 8.9 %all-to-all-start.2 = ((bf16[16,32,3584]{2,1,0:T(8,128)(2,1)}), bf16[16,32,3584]{2,1,0:T(8,128)(2,1)}, u32[]{:S(2)}, u32[]{:S(2)}) async-start(bf16[16,32,3584]{2,1,0:T(8,128)(2,1)} %get-tuple-element.30), calls=%async_computation.2 | async-start | bytes 7340032 | tf_op jit(solution)/shard_map/all_to_all | solution.py:55
  45.3 0.7 all-gather.6.cloned.1.call-update
  46.0 70.6 %all-to-all-done.2 = bf16[16,32,3584]{2,1,0:T(8,128)(2,1)} async-done(((bf16[16,32,3584]{2,1,0:T(8,128)(2,1)}), bf16[16,32,3584]{2,1,0:T(8,128)(2,1)}, u32[]{:S(2)}, u32[]{:S(2)}) %all-to-all-start.2) | async-done | bytes 3670048 | tf_op jit(solution)/shard_map/all_to_all | solution.py:55
  116.7 1.8 collective-permute-start.1
  118.5 0.1 all_to_all.25
  118.6 11.5 %all_to_all.31 = bf16[16,1,32]{2,1,0:T(2,128)(2,1)S(1)} all-to-all(bf16[16,1,32]{2,1,0:T(2,128)(2,1)S(1)} %all_to_all.25), channel_id=1, replica_groups=mesh['expert'=4,'seq'=4,'tx'=4,'core'=2] {'expert','seq'}, dimensions={0} | all-to-all | bytes 2048 | tf_op jit(solution)/shard_map/all_to_all | solution.py:57
  130.1 4.5 all-to-all-start.1
  134.7 0.7 all-gather.4.cloned.1.call-update
  135.5 64.9 %all-to-all-done.1 = bf16[16,32,3584]{2,1,0:T(8,128)(2,1)} async-done(((bf16[16,32,3584]{2,1,0:T(8,128)(2,1)}), bf16[16,32,3584]{2,1,0:T(8,128)(2,1)}, u32[]{:S(2)}, u32[]{:S(2)}) %all-to-all-start.1) | async-done | bytes 3670048 | tf_op jit(solution)/shard_map/all_to_all | solution.py:56
  200.5 6.6 %collective-permute-start = (bf16[16,32,3584]{2,1,0:T(8,128)(2,1)}, bf16[16,32,3584]{2,1,0:T(8,128)(2,1)}, u32[]{:S(2)}, u32[]{:S(2)}) collective-permute-start(bf16[16,32,3584]{2,1,0:T(8,128)(2,1)} %all-to-all-done.1), channel_id=1, source_target_pairs={{0,1},{1,0},{2,3},{3,2},{4,5},{5,4},{6,7},{7,6},{8,9},{9,8},{10,11... | collective-permute-start | bytes 11010056 | tf_op jit(solution)/shard_map/ppermute | solution.py:61
  207.0 5.4 %broadcast_select_fusion.1 = (bf16[16,32,3584]{2,1,0:T(8,128)(2,1)S(1)}, bf16[16,32,3584]{2,1,0:T(8,128)(2,1)}) fusion(bf16[16,32,3584]{2,1,0:T(8,128)(2,1)} %all-to-all-done.2, bf16[16,32,3584]{2,1,0:T(8,128)(2,1)} %collective-permute-done.1, pred[]{:T(512)S(6)} %eq.42), kind=kLoop, calls=%fused_computation.29 | loop fusion | flops 3670016 | bytes 14680065 | tf_op jit(solution)/shard_map/jit(_where)/select_n | solution.py:62
  212.5 5.8 %pad_maximum_fusion.1 = bf16[16,32,7168]{2,1,0:T(8,128)(2,1)} fusion(bf16[16,32,3584]{2,1,0:T(8,128)(2,1)} %get-tuple-element.25, bf16[16,32,3584]{2,1,0:T(8,128)(2,1)S(1)} %get-tuple-element.24), kind=kLoop, calls=%fused_computation.16 | loop fusion | flops 14680064 | bytes 14680064 | tf_op jit(solution)/shard_map/concatenate | solution.py:64
  218.2 6.2 %fusion.7 = f32[512,256]{0,1:T(8,128)S(1)} fusion(bf16[512,7168]{1,0:T(8,128)(2,1)} %bitcast.67, bf16[1,7168,256]{2,1,0:T(8,128)(2,1)} %all-gather.8.cloned.1.call-done), kind=kOutput, calls=%fused_computation.21 | convolution fusion | flops 1879048192 | bytes 11534336 | tf_op jit(solution)/shard_map/emd,edf->emf/dot_general | solution.py:87
  224.5 6.2 %fusion.10 = f32[512,256]{0,1:T(8,128)S(1)} fusion(bf16[512,7168]{1,0:T(8,128)(2,1)} %bitcast.68, bf16[1,7168,256]{2,1,0:T(8,128)(2,1)} %all-gather.6.cloned.1.call-done), kind=kOutput, calls=%fused_computation.24 | convolution fusion | flops 1879048192 | bytes 11534336 | tf_op jit(solution)/shard_map/emd,edf->emf/dot_general | solution.py:88
  230.7 5.6 %broadcast_select_fusion.3 = (bf16[16,32,3584]{2,1,0:T(8,128)(2,1)S(1)}, bf16[16,32,3584]{2,1,0:T(8,128)(2,1)}) fusion(bf16[16,32,3584]{2,1,0:T(8,128)(2,1)} %all-to-all-done.1, bf16[16,32,3584]{2,1,0:T(8,128)(2,1)} %collective-permute-done, pred[]{:T(512)S(6)} %eq.42), kind=kLoop, calls=%fused_computation.31 | loop fusion | flops 3670016 | bytes 14680065 | tf_op jit(solution)/shard_map/jit(_where)/select_n | solution.py:62
  236.3 5.8 %pad_maximum_fusion = bf16[16,32,7168]{2,1,0:T(8,128)(2,1)} fusion(bf16[16,32,3584]{2,1,0:T(8,128)(2,1)} %get-tuple-element.23, bf16[16,32,3584]{2,1,0:T(8,128)(2,1)S(1)} %get-tuple-element.22), kind=kLoop, calls=%fused_computation.15 | loop fusion | flops 14680064 | bytes 14680064 | tf_op jit(solution)/shard_map/concatenate | solution.py:64
  242.1 6.6 %multiply_reduce_fusion = (f32[512]{0:T(512)S(1)}, bf16[512,256]{0,1:T(8,128)(2,1)S(1)}, bf16[512,256]{0,1:T(8,128)(2,1)S(1)}) fusion(f32[512,256]{0,1:T(8,128)S(1)} %fusion.10, f32[512,256]{0,1:T(8,128)S(1)} %fusion.7, f32[512]{0:T(512)S(1)} %reshape.300, bf16[512,7168]{1,0:T(8,128)(2,1)} %bitcast.75, bf16[1,7168,256]{2,1,0:T(8,128)(2,1)} %all-gather.4.cloned.1.call-done), kind=kOutput, calls=%fused_computation.36 | convolution fusion | flops 1881275904 | bytes 12587008 | tf_op jit(solution)/shard_map/emd,edf->emf/dot_general | solution.py:93
  248.7 7.3 %fusion.5 = f32[512,7168]{1,0:T(8,128)} fusion(bf16[512,256]{0,1:T(8,128)(2,1)S(1)} %get-tuple-element.27, bf16[1,7168,256]{2,1,0:T(8,128)(2,1)S(1)} %copy-done.1), kind=kOutput, calls=%fused_computation.19 | convolution fusion | flops 1879048192 | bytes 18612224 | tf_op jit(solution)/shard_map/emf,edf->emd/dot_general | solution.py:101
  256.0 10.6 %fusion = bf16[1,512,7168]{2,1,0:T(8,128)(2,1)} fusion(f32[512,7168]{1,0:T(8,128)} %fusion.5, bf16[512,256]{0,1:T(8,128)(2,1)S(1)} %get-tuple-element.28, bf16[1,7168,256]{2,1,0:T(8,128)(2,1)S(1)} %copy-done), kind=kOutput, calls=%fused_computation.8 | convolution fusion | flops 1886388224 | bytes 25952256 | tf_op jit(solution)/shard_map/emf,edf->emd/dot_general | solution.py:104
  266.6 31.4 %copy.30 = bf16[1,512,7168]{1,0,2:T(2,128)(2,1)} copy(bf16[1,512,7168]{2,1,0:T(8,128)(2,1)} %fusion) | data formatting | bytes 14680064
  298.1 10.3 %copy.36 = bf16[7168,1,512]{2,0,1:T(8,128)(2,1)} copy(bf16[7168,1,512]{2,1,0:T(2,128)(2,1)} %bitcast.71) | data formatting | bytes 14680064
  308.5 8.0 %fusion.3 = bf16[1,7168,256]{2,1,0:T(8,128)(2,1)} fusion(bf16[512,7168]{1,0:T(8,128)(2,1)} %bitcast.76, f32[512]{0:T(512)S(1)} %reshape.300, f32[512,256]{0,1:T(8,128)S(1)} %fusion.10, f32[512,256]{0,1:T(8,128)S(1)} %fusion.7), kind=kOutput, calls=%fused_computation.14 | convolution fusion | flops 1892679680 | bytes 12060672 | tf_op jit(solution)/shard_map/emd,emf->edf/dot_general | solution.py:132
  316.6 7.1 %fusion.1 = bf16[1,7168,256]{2,1,0:T(8,128)(2,1)} fusion(bf16[512,7168]{1,0:T(8,128)(2,1)} %bitcast.69, bf16[512,256]{0,1:T(8,128)(2,1)S(1)} %get-tuple-element.27), kind=kOutput, calls=%fused_computation.12 | convolution fusion | flops 1880883200 | bytes 11272192 | tf_op jit(solution)/shard_map/emd,emf->edf/dot_general | solution.py:130
  323.8 7.2 %fusion.2 = bf16[1,7168,256]{2,1,0:T(8,128)(2,1)} fusion(bf16[512,7168]{1,0:T(8,128)(2,1)} %bitcast.70, bf16[512,256]{0,1:T(8,128)(2,1)S(1)} %get-tuple-element.28), kind=kOutput, calls=%fused_computation.13 | convolution fusion | flops 1880883200 | bytes 11272192 | tf_op jit(solution)/shard_map/emd,emf->edf/dot_general | solution.py:131
  330.9 9.4 %psum.14 = f32[1,512]{1,0:T(1,128)S(1)} all-reduce(f32[1,512]{1,0:T(1,128)S(1)} %bitcast.78), channel_id=1, replica_groups=mesh['expert'=4,'seq'=4,'tx'=4,'core'=2] {'tx'}, use_global_device_ids=true, to_apply=%region_7.8 | all-reduce | flops 512 | bytes 4096 | tf_op jit(solution)/shard_map/psum | solution.py:11
  340.3 4.7 psum.15
  345.1 0.7 convert_element_type.144
  345.8 3.7 all-to-all-start.4
  349.4 2.7 reduce-scatter.13.cloned.1.call-done
  352.1 2.1 reshape_bitcast_fusion
  354.3 3.4 copy.31
  357.7 6.7 %all-to-all-start.3 = ((bf16[16,32,896]{2,1,0:T(8,128)(2,1)}), bf16[16,32,896]{2,1,0:T(8,128)(2,1)S(1)}, u32[]{:S(2)}, u32[]{:S(2)}) async-start(bf16[16,32,896]{2,1,0:T(8,128)(2,1)} %bitcast.9), calls=%async_computation.3 | async-start | bytes 1835008 | tf_op jit(solution)/shard_map/all_to_all | solution.py:112
  364.5 2.8 gather_fusion.4
  367.3 0.1 reshape.299
  367.4 0.7 copy.29
  368.1 39.1 %reduce-scatter.11.cloned.1.call-done = bf16[1,1792,256]{2,1,0:T(8,128)(2,1)} async-done(((bf16[1,7168,256]{2,1,0:T(8,128)(2,1)}), bf16[1,1792,256]{2,1,0:T(8,128)(2,1)}) %reduce-scatter.11.cloned.1.call-update) | async-done | bytes 917520 | tf_op jit(solution)/shard_map/reduce_scatter | solution.py:140
  407.2 2.5 convert_element_type.141
  409.7 42.0 %reduce-scatter.7.cloned.1.call-done = bf16[1,1792,256]{2,1,0:T(8,128)(2,1)} async-done(((bf16[1,7168,256]{2,1,0:T(8,128)(2,1)}), bf16[1,1792,256]{2,1,0:T(8,128)(2,1)}) %reduce-scatter.7.cloned.1.call-update) | async-done | bytes 917520 | tf_op jit(solution)/shard_map/reduce_scatter | solution.py:134
  451.7 2.5 convert_element_type.132
  454.3 42.1 %reduce-scatter.9.cloned.1.call-done = bf16[1,1792,256]{2,1,0:T(8,128)(2,1)} async-done(((bf16[1,7168,256]{2,1,0:T(8,128)(2,1)}), bf16[1,1792,256]{2,1,0:T(8,128)(2,1)}) %reduce-scatter.9.cloned.1.call-update) | async-done | bytes 917520 | tf_op jit(solution)/shard_map/reduce_scatter | solution.py:137
  496.4 2.5 convert_element_type.135
  499.0 0.2 bitcast_convert_fusion
  499.2 1.9 gather_fusion.3
  501.1 0.8 reshape.298
  501.9 2.5 reduce_sum.33
  (37 shorter events, 0.8 us)
Async XLA Ops:
  7.2 211.1 %all-gather.8.cloned.1.call-start = ((), (), s32[]{:S(2)}) async-start(), calls=%async_computation.11 | async-start | bytes 4587520 | tf_op jit(solution)/shard_map/all_gather | solution.py:83
  36.4 80.3 %all-to-all-start.2 = ((bf16[16,32,3584]{2,1,0:T(8,128)(2,1)}), bf16[16,32,3584]{2,1,0:T(8,128)(2,1)}, u32[]{:S(2)}, u32[]{:S(2)}) async-start(bf16[16,32,3584]{2,1,0:T(8,128)(2,1)} %get-tuple-element.30), calls=%async_computation.2 | async-start | bytes 7340032 | tf_op jit(solution)/shard_map/all_to_all | solution.py:55
  45.3 179.2 %all-gather.6.cloned.1.call-start = ((), (), s32[]{:S(2)}) async-start(), calls=%async_computation.10 | async-start | bytes 4587520 | tf_op jit(solution)/shard_map/all_gather | solution.py:84
  116.7 90.4 %collective-permute-start.1 = (bf16[16,32,3584]{2,1,0:T(8,128)(2,1)}, bf16[16,32,3584]{2,1,0:T(8,128)(2,1)}, u32[]{:S(2)}, u32[]{:S(2)}) collective-permute-start(bf16[16,32,3584]{2,1,0:T(8,128)(2,1)} %all-to-all-done.2), channel_id=1, source_target_pairs={{0,1},{1,0},{2,3},{3,2},{4,5},{5,4},{6,7},{7,6},{8,9},{9,8},{10,11... | collective-permute-start | bytes 11010056 | tf_op jit(solution)/shard_map/ppermute | solution.py:61
  130.1 70.3 %all-to-all-start.1 = ((bf16[16,32,3584]{2,1,0:T(8,128)(2,1)}), bf16[16,32,3584]{2,1,0:T(8,128)(2,1)}, u32[]{:S(2)}, u32[]{:S(2)}) async-start(bf16[16,32,3584]{2,1,0:T(8,128)(2,1)} %get-tuple-element.29), calls=%async_computation.1 | async-start | bytes 7340032 | tf_op jit(solution)/shard_map/all_to_all | solution.py:56
  134.6 107.4 %all-gather.4.cloned.1.call-start = ((), (), s32[]{:S(2)}) async-start(), calls=%async_computation.9 | async-start | bytes 4587520 | tf_op jit(solution)/shard_map/all_gather | solution.py:85
  135.4 216.8 %reduce-scatter.13.cloned.1.call-start = ((), (), s32[]{:S(2)}) async-start(), calls=%async_computation.15 | async-start | bytes 8257536
  200.5 30.3 %collective-permute-start = (bf16[16,32,3584]{2,1,0:T(8,128)(2,1)}, bf16[16,32,3584]{2,1,0:T(8,128)(2,1)}, u32[]{:S(2)}, u32[]{:S(2)}) collective-permute-start(bf16[16,32,3584]{2,1,0:T(8,128)(2,1)} %all-to-all-done.1), channel_id=1, source_target_pairs={{0,1},{1,0},{2,3},{3,2},{4,5},{5,4},{6,7},{7,6},{8,9},{9,8},{10,11... | collective-permute-start | bytes 11010056 | tf_op jit(solution)/shard_map/ppermute | solution.py:61
  242.1 6.6 %copy-start.1 = (bf16[1,7168,256]{2,1,0:T(8,128)(2,1)S(1)}, bf16[1,7168,256]{2,1,0:T(8,128)(2,1)}, u32[]{:S(2)}) copy-start(bf16[1,7168,256]{2,1,0:T(8,128)(2,1)} %all-gather.8.cloned.1.call-done) | copy-start | bytes 11010052
  248.7 7.4 %copy-start = (bf16[1,7168,256]{2,1,0:T(8,128)(2,1)S(1)}, bf16[1,7168,256]{2,1,0:T(8,128)(2,1)}, u32[]{:S(2)}) copy-start(bf16[1,7168,256]{2,1,0:T(8,128)(2,1)} %all-gather.6.cloned.1.call-done) | copy-start | bytes 11010052
  308.4 98.8 %reduce-scatter.11.cloned.1.call-start = ((), (), s32[]{:S(2)}) async-start(), calls=%async_computation.14 | async-start | bytes 4587520 | tf_op jit(solution)/shard_map/reduce_scatter | solution.py:140
  316.5 135.2 %reduce-scatter.7.cloned.1.call-start = ((), (), s32[]{:S(2)}) async-start(), calls=%async_computation.12 | async-start | bytes 4587520 | tf_op jit(solution)/shard_map/reduce_scatter | solution.py:134
  323.7 172.7 %reduce-scatter.9.cloned.1.call-start = ((), (), s32[]{:S(2)}) async-start(), calls=%async_computation.13 | async-start | bytes 4587520 | tf_op jit(solution)/shard_map/reduce_scatter | solution.py:137
  345.8 11.9 %all-to-all-start.4 = ((bf16[16,1,32]{2,1,0:T(2,128)(2,1)}), bf16[16,1,32]{2,1,0:T(2,128)(2,1)S(1)}, u32[]{:S(2)}, u32[]{:S(2)}) async-start(bf16[16,1,32]{2,1,0:T(2,128)(2,1)} %convert_element_type.144), calls=%async_computation.4 | async-start | bytes 16384 | tf_op jit(solution)/shard_map/all_to_all | solution.py:119
  357.7 141.3 %all-to-all-start.3 = ((bf16[16,32,896]{2,1,0:T(8,128)(2,1)}), bf16[16,32,896]{2,1,0:T(8,128)(2,1)S(1)}, u32[]{:S(2)}, u32[]{:S(2)}) async-start(bf16[16,32,896]{2,1,0:T(8,128)(2,1)} %bitcast.9), calls=%async_computation.3 | async-start | bytes 1835008 | tf_op jit(solution)/shard_map/all_to_all | solution.py:112
Sparse Core Ops, SparseCore 0:
  9.7 68.7 all-gather.7
  80.2 55.4 all-gather.5
  137.3 70.2 all-gather.3
  308.6 43.5 reduce-scatter.12
  354.4 52.7 reduce-scatter.10
  409.5 42.2 reduce-scatter.6
  454.2 42.2 reduce-scatter.8
